TPU v7x, 32 devices: a whole 2x2x4 slice. The times are simulated.
32 devices in a mesh: dp: 2 (over y), head: 4 (over z), tensor: 4 (over x, core).
Axes of the slice: x: 2, y: 2, z: 4, core: 2. Of those that a mesh axis runs over, the one named last changes fastest.
Arguments:
- tokens: bfloat16 [512, 8192], P('dp', 'tensor'), may hold values from -6 to 6
- cotangent: bfloat16 [512, 8192], P('dp', 'tensor'), may hold values from -6 to 6
- w_gate: bfloat16 [8192, 29568], P('tensor', 'head'), may hold values from -0.0625 to 0.0625
- w_up: bfloat16 [8192, 29568], P('tensor', 'head'), may hold values from -0.0625 to 0.0625
- w_down: bfloat16 [29568, 8192], P('head', 'tensor'), may hold values from -0.03125 to 0.03125
- common_down_factor: bfloat16 [8192, 64], P('tensor'), may hold values from -0.0625 to 0.0625
- head_up: bfloat16 [64, 64, 8192], P('head', None, 'tensor'), may hold values from -0.0625 to 0.0625
- routes: int32 [512, 1], P('dp'), may hold values from 0 to 63
Outputs:
- grad_x: bfloat16 [512, 8192], P(('dp', 'head'), 'tensor')
- grad_shared: float32 [8192, 64], P('tensor')
- up_head_gradients: float32 [64, 64, 8192], P('head', None, 'tensor')
Inputs may be any that keep to these rules, and one draw needn't show every extreme that they name: `routes`: each token names one adapter head; the loads are skewed.
All inputs are finite; a program needn't handle non-finite values.
Results may differ from a plain program's by a relative error of at most 0.015.
Values may be sent and summed in bfloat16 or wider, within the bound.
No kernel may reach another device: no remote copies, remote signals or barrier semaphores. Data moves between devices by JAX's collectives and lax.ppermute only.
A program may use at most 256 MiB of HBM per device.

v0:
```python
import jax
import jax.numpy as jnp
from jax import lax
from jax.sharding import PartitionSpec as P

ADAPTER_SCALE = 2.0


def contract_last(left, right):
    return lax.dot_general(
        left, right, (((1,), (1,)), ((), ())), preferred_element_type=jnp.float32
    )


def local(tokens, cotangent, w_gate, w_up, w_down, common_down_factor, head_up, routes):
    tok_rows, d_cols = tokens.shape
    hidden_activation = w_gate.shape[1]
    reduced_activation = common_down_factor.shape[1]
    local_heads = head_up.shape[0]
    first_head = lax.axis_index("head") * local_heads
    assigned_mask = (
        routes == first_head + jnp.arange(local_heads, dtype=jnp.int32)[None, :]
    ).astype(jnp.float32)
    flat_heads = head_up.reshape(local_heads * reduced_activation, d_cols)
    gate_preactivation = jnp.dot(tokens, w_gate, preferred_element_type=jnp.float32)
    up_preactivation = jnp.dot(tokens, w_up, preferred_element_type=jnp.float32)
    returned_gradient = contract_last(cotangent, w_down)
    adapter_selectors = jnp.dot(tokens, common_down_factor, preferred_element_type=jnp.float32)
    head_separated = contract_last(cotangent, flat_heads).reshape(
        tok_rows // lax.axis_size("tensor") * lax.axis_size("tensor"),
        local_heads,
        reduced_activation,
    )
    selector_gradient = ADAPTER_SCALE * jnp.sum(head_separated * assigned_mask[:, :, None], axis=1)
    shared_rows = lax.psum_scatter(
        jnp.concatenate(
            [
                gate_preactivation,
                up_preactivation,
                returned_gradient,
                adapter_selectors,
                selector_gradient,
            ],
            axis=1,
        ),
        "tensor",
        scatter_dimension=0,
        tiled=True,
    )
    gate_preactivation = shared_rows[:, :hidden_activation]
    up_preactivation = shared_rows[:, hidden_activation : 2 * hidden_activation]
    returned_gradient = shared_rows[:, 2 * hidden_activation : 3 * hidden_activation]
    adapter_selectors = shared_rows[
        :, 3 * hidden_activation : 3 * hidden_activation + reduced_activation
    ].astype(jnp.bfloat16)
    selector_gradient = shared_rows[:, 3 * hidden_activation + reduced_activation :].astype(
        jnp.bfloat16
    )
    sig_gate = jax.nn.sigmoid(gate_preactivation)
    gate_gradient = (
        returned_gradient
        * up_preactivation
        * sig_gate
        * (1.0 + gate_preactivation * (1.0 - sig_gate))
    ).astype(jnp.bfloat16)
    up_gradient = (returned_gradient * gate_preactivation * sig_gate).astype(jnp.bfloat16)
    gate_gradient, up_gradient, adapter_selectors, selector_gradient = (
        gate_gradient,
        up_gradient,
        adapter_selectors,
        selector_gradient,
    )
    packed = jnp.concatenate(
        [gate_gradient, up_gradient, adapter_selectors, selector_gradient], axis=1
    )
    part_rows = lax.all_gather(packed, "tensor", axis=0, tiled=True)
    ffn_rows = contract_last(part_rows[:, :hidden_activation], w_gate) + contract_last(
        part_rows[:, hidden_activation : 2 * hidden_activation], w_up
    )
    gathered = jnp.concatenate(
        [ffn_rows, part_rows[:, 2 * hidden_activation :].astype(jnp.float32)], axis=1
    )
    ffn_part = gathered[:, :d_cols]
    adapter_selectors = gathered[:, d_cols : d_cols + reduced_activation].astype(jnp.bfloat16)
    selector_gradient = gathered[:, d_cols + reduced_activation :].astype(jnp.bfloat16)
    own_ffn, own_code = (
        lax.psum_scatter(ffn_part, "head", scatter_dimension=0, tiled=True),
        lax.psum_scatter(
            selector_gradient.astype(jnp.float32), "head", scatter_dimension=0, tiled=True
        ),
    )
    grad_x = (own_ffn + contract_last(own_code.astype(jnp.bfloat16), common_down_factor)).astype(
        jnp.bfloat16
    )
    selector_mask = (
        adapter_selectors[:, None, :] * assigned_mask[:, :, None].astype(jnp.bfloat16)
    ).reshape(tok_rows, local_heads * reduced_activation)
    head_contributions = ADAPTER_SCALE * lax.dot_general(
        selector_mask, cotangent, (((0,), (0,)), ((), ())), preferred_element_type=jnp.float32
    )
    up_head_gradients = lax.psum(
        head_contributions.reshape(local_heads, reduced_activation, d_cols).astype(jnp.bfloat16),
        "dp",
    ).astype(jnp.float32)
    shared_term = lax.dot_general(
        tokens, selector_gradient, (((0,), (0,)), ((), ())), preferred_element_type=jnp.float32
    )
    grad_shared = lax.psum(shared_term.astype(jnp.bfloat16), ("dp", "head")).astype(jnp.float32)
    return (grad_x, grad_shared, up_head_gradients)


def solution(mesh):
    placed = (
        P("dp", "tensor"),
        P("dp", "tensor"),
        P("tensor", "head"),
        P("tensor", "head"),
        P("head", "tensor"),
        P("tensor", None),
        P("head", None, "tensor"),
        P("dp", None),
    )
    return jax.shard_map(
        local,
        mesh=mesh,
        in_specs=placed,
        out_specs=(P(("dp", "head"), "tensor"), P("tensor", None), P("head", None, "tensor")),
        check_vma=False,
    )
```

profile of v0, /device:TPU:0, one launch (start us, length us, event | category | flops | bytes accessed | tf_op | source)
XLA Modules:
  0.0 568.6 jit_solution(10104915546490771158)
XLA Ops:
  7.2 0.0 copy-start
  7.2 0.0 reduce-scatter.10.cloned.1.call-start
  7.2 0.8 fusion.15
  8.1 0.3 copy-done
  8.4 15.7 %convolution_dynamic-update-slice_fusion.2 = f32[256,22304]{0,1:T(8,128)} fusion(bf16[256,2048]{1,0:T(8,128)(2,1)S(1)} %copy-done, bf16[2048,7392]{0,1:T(8,128)(2,1)} %param.10), kind=kOutput, calls=%fused_computation.2 | convolution fusion | flops 7751073792 | bytes 38895616 | tf_op jit(solution)/shard_map/dot_general | solution.py:25
  24.1 0.0 copy-start.2
  24.1 0.0 copy-start.3
  24.1 15.9 %convolution_dynamic-update-slice_fusion.1 = f32[256,22304]{0,1:T(8,128)} fusion(f32[256,22304]{0,1:T(8,128)} %convolution_dynamic-update-slice_fusion.2, bf16[256,2048]{1,0:T(8,128)(2,1)S(1)} %copy-done, bf16[2048,7392]{0,1:T(8,128)(2,1)} %param.11), kind=kOutput, calls=%fused_computation.1 | convolution fusion | flops 7751073792 | bytes 38895616 | tf_op jit(solution)/shard_map/dot_general | solution.py:26
  40.0 0.0 copy-done.2
  40.0 0.0 copy-done.3
  40.0 1.3 fusion.12
  41.3 0.0 copy-start.1
  41.3 15.8 %convolution_dynamic-update-slice_fusion = f32[256,22304]{0,1:T(8,128)} fusion(f32[256,22304]{0,1:T(8,128)} %convolution_dynamic-update-slice_fusion.1, bf16[256,2048]{1,0:T(8,128)(2,1)S(1)} %copy-done.3, bf16[7392,2048]{1,0:T(8,128)(2,1)} %param.12), kind=kOutput, calls=%fused_computation | convolution fusion | flops 7751073792 | bytes 38895616 | tf_op jit(solution)/shard_map/dot_general | solution.py:10
  57.1 0.0 copy-done.1
  57.1 1.1 convolution_dynamic-update-slice_fusion.3
  58.2 0.6 multiply_dynamic-update-slice_fusion
  58.8 23.2 %copy.22 = f32[256,22304]{1,0:T(8,128)} copy(f32[256,22304]{0,1:T(8,128)} %multiply_dynamic-update-slice_fusion) | data formatting | bytes 45678592
  82.0 0.0 reduce-scatter.10.cloned.1.call-update
  82.1 0.0 all-gather.2.cloned.1.call-start
  82.1 165.1 %reduce-scatter.10.cloned.1.call-done = f32[64,22304]{1,0:T(8,128)} async-done(((f32[256,22304]{1,0:T(8,128)}), f32[64,22304]{1,0:T(8,128)}) %reduce-scatter.10.cloned.1.call-update) | async-done | bytes 5709840 | tf_op jit(solution)/shard_map/reduce_scatter | solution.py:35
  247.2 0.9 slice.72
  248.1 3.7 multiply_convert_fusion.1
  251.9 2.4 concatenate.7
  254.3 0.0 all-gather.2.cloned.1.call-update
  254.3 0.0 reduce-scatter.12.cloned.1.call-start
  254.3 54.3 %all-gather.2.cloned.1.call-done = bf16[256,14912]{1,0:T(8,128)(2,1)} async-done(((bf16[64,14912]{1,0:T(8,128)(2,1)}), bf16[256,14912]{1,0:T(8,128)(2,1)}) %all-gather.2.cloned.1.call-update) | async-done | bytes 7634960 | tf_op jit(solution)/shard_map/all_gather | solution.py:76
  308.6 1.0 fusion.17
  309.6 0.1 copy.21
  309.7 0.1 copy.26
  309.8 0.8 copy.24
  310.5 0.0 reduce-scatter.12.cloned.1.call-update
  310.5 0.0 all-reduce.3.cloned.1.call-start
  310.6 1.9 fusion.8
  312.5 0.0 all-reduce.3.cloned.1.call-update
  312.5 0.0 all-reduce.5.cloned.1.call-start
  312.6 4.5 multiply_convert_fusion
  317.1 0.0 all-reduce.5.cloned.1.call-update
  317.1 0.0 reduce-scatter.8.cloned.1.call-start
  317.2 15.2 %fusion = f32[256,2048]{1,0:T(8,128)S(1)} fusion(bf16[2048,7392]{0,1:T(8,128)(2,1)} %param.11, bf16[256,14912]{1,0:T(8,128)(2,1)} %all-gather.2.cloned.1.call-done), kind=kOutput, calls=%fused_computation.4 | convolution fusion | flops 7751073792 | bytes 36175872 | tf_op jit(solution)/shard_map/dot_general | solution.py:10
  332.3 15.9 %fusion.4 = f32[256,2048]{1,0:T(8,128)} fusion(f32[256,2048]{1,0:T(8,128)S(1)} %fusion, bf16[2048,7392]{0,1:T(8,128)(2,1)} %param.10, bf16[256,14912]{1,0:T(8,128)(2,1)} %all-gather.2.cloned.1.call-done), kind=kOutput, calls=%fused_computation.8 | convolution fusion | flops 7751598080 | bytes 38273024 | tf_op jit(solution)/shard_map/dot_general | solution.py:10
  348.2 0.0 reduce-scatter.8.cloned.1.call-update
  348.2 0.0 reduce-scatter.12.cloned.1.call-done
  348.3 0.8 copy.25
  349.1 54.8 %all-reduce.3.cloned.1.call-done = bf16[2048,64]{0,1:T(8,128)(2,1)} async-done(((bf16[2048,64]{0,1:T(8,128)(2,1)}), bf16[2048,64]{0,1:T(8,128)(2,1)}) %all-reduce.3.cloned.1.call-update) | async-done | bytes 262160 | tf_op jit(solution)/shard_map/psum | solution.py:108
  403.9 1.8 convert_element_type.64
  405.7 108.2 %all-reduce.5.cloned.1.call-done = bf16[16,64,2048]{2,1,0:T(8,128)(2,1)} async-done(((bf16[16,64,2048]{2,1,0:T(8,128)(2,1)}), bf16[16,64,2048]{2,1,0:T(8,128)(2,1)}) %all-reduce.5.cloned.1.call-update) | async-done | bytes 4194320 | tf_op jit(solution)/shard_map/psum | solution.py:101
  513.9 6.7 %convert_element_type.68 = f32[16,64,2048]{2,1,0:T(8,128)} convert(bf16[16,64,2048]{2,1,0:T(8,128)(2,1)} %all-reduce.5.cloned.1.call-done) | non-fusion elementwise | flops 2097152 | bytes 12582912 | tf_op jit(solution)/shard_map/convert_element_type | solution.py:104
  520.6 39.2 %reduce-scatter.8.cloned.1.call-done = f32[64,2048]{1,0:T(8,128)} async-done(((f32[256,2048]{1,0:T(8,128)}), f32[64,2048]{1,0:T(8,128)}) %reduce-scatter.8.cloned.1.call-update) | async-done | bytes 524304 | tf_op jit(solution)/shard_map/reduce_scatter | solution.py:87
  559.7 2.0 fusion.7
  (2 shorter events, 0.0 us)
Async XLA Ops:
  7.2 1.2 copy-start
  7.2 240.0 %reduce-scatter.10.cloned.1.call-start = ((), (), s32[]{:S(2)}) async-start(), calls=%async_computation.7 | async-start | bytes 28672000 | tf_op jit(solution)/shard_map/reduce_scatter | solution.py:35
  24.1 15.9 %copy-start.2 = (bf16[16,64,2048]{2,1,0:T(8,128)(2,1)S(1)}, bf16[16,64,2048]{2,1,0:T(8,128)(2,1)}, u32[]{:S(2)}) copy-start(bf16[16,64,2048]{2,1,0:T(8,128)(2,1)} %param.14) | copy-start | bytes 12582916
  24.1 15.9 %copy-start.3 = (bf16[256,2048]{1,0:T(8,128)(2,1)S(1)}, bf16[256,2048]{1,0:T(8,128)(2,1)}, u32[]{:S(2)}) copy-start(bf16[256,2048]{1,0:T(8,128)(2,1)} %param.9) | copy-start | bytes 3145732
  41.3 15.8 %copy-start.1 = (bf16[2048,64]{0,1:T(8,128)(2,1)S(1)}, bf16[2048,64]{0,1:T(8,128)(2,1)}, u32[]{:S(2)}) copy-start(bf16[2048,64]{0,1:T(8,128)(2,1)} %param.13) | copy-start | bytes 786436
  82.1 226.5 %all-gather.2.cloned.1.call-start = ((), (), s32[]{:S(2)}) async-start(), calls=%async_computation.3 | async-start | bytes 9584640 | tf_op jit(solution)/shard_map/all_gather | solution.py:76
  254.3 94.0 %reduce-scatter.12.cloned.1.call-start = ((), (), s32[]{:S(2)}) async-start(), calls=%async_computation.8 | async-start | bytes 163840
  310.5 93.3 %all-reduce.3.cloned.1.call-start = ((), (), s32[]{:S(2)}) async-start(), calls=%async_computation.5 | async-start | bytes 524288 | tf_op jit(solution)/shard_map/psum | solution.py:108
  312.5 201.4 %all-reduce.5.cloned.1.call-start = ((), (), s32[]{:S(2)}) async-start(), calls=%async_computation.6 | async-start | bytes 8388608 | tf_op jit(solution)/shard_map/psum | solution.py:101
  317.1 242.6 %reduce-scatter.8.cloned.1.call-start = ((), (), s32[]{:S(2)}) async-start(), calls=%async_computation.4 | async-start | bytes 2621440 | tf_op jit(solution)/shard_map/reduce_scatter | solution.py:87
Sparse Core Ops, SparseCore 0:
  82.2 164.9 reduce-scatter.9
  254.4 54.1 all-gather.1
  311.4 19.4 reduce-scatter.11
  334.7 69.1 all-reduce.2
  406.7 107.1 all-reduce.4
  516.0 43.6 reduce-scatter.7
where the time goes:
time: 569 us
  waiting for transfers between devices  422 us (74%)
  matrix products  89.2 us (16%)
  local copies, waits for them, and re-layouts  29.6 us (5%)
  between operations  14.2 us (2%)
  other arithmetic  13.7 us (2%)
    reduce_scatter x1, waiting for transfers between devices, local(): lax.psum_scatter(jnp.concatenate([gate_preactivation, up_preactivation, r...  165 us
    psum x1, waiting for transfers between devices, local(): lax.psum(head_contributions.reshape(local_heads, reduced_activation, d_co...  108 us
    psum x1, waiting for transfers between devices, local(): lax.psum(shared_term.astype(jnp.bfloat16), ('dp', 'head'))  54.8 us
    all_gather x1, waiting for transfers between devices, local(): part_rows = lax.all_gather(packed, 'tensor', axis=0, tiled=True)  54.3 us
    dot_general x5, matrix products, contract_last(): lax.dot_general(left, right, (((1,), (1,)), ((), ())), preferred_element_...  50.1 us
    reduce_scatter x1, waiting for transfers between devices, local(): lax.psum_scatter(ffn_part, 'head', scatter_dimension=0, tiled=True)  39.2 us
    unnamed x12, local copies, waits for them, and re-layouts  25.3 us
    dot_general x1, matrix products, local(): up_preactivation = jnp.dot(tokens, w_up, preferred_element_type=jnp.float32)  15.9 us
  transfers between devices with their start and end apart: 6, of which 5 were waited for; matrix products, arithmetic and copies ran while one was open for 8% of the time, Pallas kernels for 0%

commit v1 on v0

--- a/solution.py
+++ b/solution.py
@@ -1,9 +1,17 @@
+import functools
 import jax
 import jax.numpy as jnp
 from jax import lax
 from jax.sharding import PartitionSpec as P
 
 ADAPTER_SCALE = 2.0
+
+
+def finish_stages_all(u_in, axis_tag):
+    return jnp.sum(lax.all_gather(u_in, axis_tag), axis=0)
+
+
+slot_unite = functools.partial(finish_stages_all, axis_tag=("dp", "head"))
 
 
 def contract_last(left, right):
@@ -105,7 +113,7 @@
     shared_term = lax.dot_general(
         tokens, selector_gradient, (((0,), (0,)), ((), ())), preferred_element_type=jnp.float32
     )
-    grad_shared = lax.psum(shared_term.astype(jnp.bfloat16), ("dp", "head")).astype(jnp.float32)
+    grad_shared = slot_unite(shared_term.astype(jnp.bfloat16)).astype(jnp.float32)
     return (grad_x, grad_shared, up_head_gradients)
 
 

time: 569 us -> 546 us (0.960)
  waiting for transfers between devices: 422 us -> 394 us
    psum x1 -> x0, waiting for transfers between devices: 54.8 us -> none  [local(): lax.psum(shared_term.astype(jnp.bfloat16), ('dp', 'head'))]
    all_gather x0 -> x1, waiting for transfers between devices: none -> 31.5 us  [finish_stages_all(): return jnp.sum(lax.all_gather(u_in, axis_tag), axis=0)]
    unnamed x12 -> x13, local copies, waits for them, and re-layouts: 25.3 us -> 28 us
  transfers between devices with their start and end apart: 6 -> 6, of which waited for: 5 -> 5; matrix products, arithmetic and copies ran while one was open for 8% -> 9% of each run, Pallas kernels for 0% -> 0%
where the time goes in v1:
time: 546 us; the launch traced here: 545 us
  waiting for transfers between devices  394 us (72%)
  matrix products  89.4 us (16%)
  local copies, waits for them, and re-layouts  32.4 us (6%)
  other arithmetic  14.3 us (3%)
  between operations  14.2 us (3%)
    reduce_scatter x1, waiting for transfers between devices, local(): lax.psum_scatter(jnp.concatenate([gate_preactivation, up_preactivation, r...  165 us
    psum x1, waiting for transfers between devices, local(): lax.psum(head_contributions.reshape(local_heads, reduced_activation, d_co...  104 us
    all_gather x1, waiting for transfers between devices, local(): part_rows = lax.all_gather(packed, 'tensor', axis=0, tiled=True)  54.3 us
    dot_general x5, matrix products, contract_last(): lax.dot_general(left, right, (((1,), (1,)), ((), ())), preferred_element_...  50.3 us
    reduce_scatter x1, waiting for transfers between devices, local(): lax.psum_scatter(ffn_part, 'head', scatter_dimension=0, tiled=True)  39.2 us
    all_gather x1, waiting for transfers between devices, finish_stages_all(): return jnp.sum(lax.all_gather(u_in, axis_tag), axis=0)  31.5 us
    unnamed x13, local copies, waits for them, and re-layouts  28 us
    dot_general x1, matrix products, local(): up_preactivation = jnp.dot(tokens, w_up, preferred_element_type=jnp.float32)  15.9 us
  transfers between devices with their start and end apart: 6, of which 5 were waited for; matrix products, arithmetic and copies ran while one was open for 9% of the time, Pallas kernels for 0%

profile of v1, /device:TPU:0, one launch (start us, length us, event | category | flops | bytes accessed | tf_op | source)
XLA Modules:
  0.0 544.8 jit_solution(9775679217820932028)
XLA Ops:
  7.2 0.0 copy-start
  7.2 0.0 reduce-scatter.10.cloned.1.call-start
  7.2 0.8 fusion.15
  8.1 0.3 copy-done
  8.4 15.7 %convolution_dynamic-update-slice_fusion.2 = f32[256,22304]{0,1:T(8,128)} fusion(bf16[256,2048]{1,0:T(8,128)(2,1)S(1)} %copy-done, bf16[2048,7392]{0,1:T(8,128)(2,1)} %param.10), kind=kOutput, calls=%fused_computation.2 | convolution fusion | flops 7751073792 | bytes 38895616 | tf_op jit(solution)/shard_map/dot_general | solution.py:33
  24.1 0.0 copy-start.2
  24.1 0.0 copy-start.3
  24.1 15.9 %convolution_dynamic-update-slice_fusion.1 = f32[256,22304]{0,1:T(8,128)} fusion(f32[256,22304]{0,1:T(8,128)} %convolution_dynamic-update-slice_fusion.2, bf16[256,2048]{1,0:T(8,128)(2,1)S(1)} %copy-done, bf16[2048,7392]{0,1:T(8,128)(2,1)} %param.11), kind=kOutput, calls=%fused_computation.1 | convolution fusion | flops 7751073792 | bytes 38895616 | tf_op jit(solution)/shard_map/dot_general | solution.py:34
  40.0 0.0 copy-done.2
  40.0 0.0 copy-done.3
  40.0 1.3 fusion.12
  41.3 0.0 copy-start.1
  41.3 15.8 %convolution_dynamic-update-slice_fusion = f32[256,22304]{0,1:T(8,128)} fusion(f32[256,22304]{0,1:T(8,128)} %convolution_dynamic-update-slice_fusion.1, bf16[256,2048]{1,0:T(8,128)(2,1)S(1)} %copy-done.3, bf16[7392,2048]{1,0:T(8,128)(2,1)} %param.12), kind=kOutput, calls=%fused_computation | convolution fusion | flops 7751073792 | bytes 38895616 | tf_op jit(solution)/shard_map/dot_general | solution.py:18
  57.1 0.0 copy-done.1
  57.1 1.1 convolution_dynamic-update-slice_fusion.3
  58.2 0.6 multiply_dynamic-update-slice_fusion
  58.8 23.2 %copy.22 = f32[256,22304]{1,0:T(8,128)} copy(f32[256,22304]{0,1:T(8,128)} %multiply_dynamic-update-slice_fusion) | data formatting | bytes 45678592
  82.0 0.0 reduce-scatter.10.cloned.1.call-update
  82.1 0.0 all-gather.4.cloned.1.call-start
  82.1 165.1 %reduce-scatter.10.cloned.1.call-done = f32[64,22304]{1,0:T(8,128)} async-done(((f32[256,22304]{1,0:T(8,128)}), f32[64,22304]{1,0:T(8,128)}) %reduce-scatter.10.cloned.1.call-update) | async-done | bytes 5709840 | tf_op jit(solution)/shard_map/reduce_scatter | solution.py:43
  247.2 0.9 slice.72
  248.1 3.7 multiply_convert_fusion.1
  251.9 2.4 concatenate.7
  254.3 0.0 all-gather.4.cloned.1.call-update
  254.3 0.0 reduce-scatter.12.cloned.1.call-start
  254.3 54.3 %all-gather.4.cloned.1.call-done = bf16[256,14912]{1,0:T(8,128)(2,1)} async-done(((bf16[64,14912]{1,0:T(8,128)(2,1)}), bf16[256,14912]{1,0:T(8,128)(2,1)}) %all-gather.4.cloned.1.call-update) | async-done | bytes 7634960 | tf_op jit(solution)/shard_map/all_gather | solution.py:84
  308.6 1.0 fusion.17
  309.6 0.1 copy.26
  309.7 0.8 copy.24
  310.4 0.0 reduce-scatter.12.cloned.1.call-update
  310.4 0.0 all-gather.6.cloned.1.call-start
  310.5 1.9 fusion.8
  312.4 0.0 all-gather.6.cloned.1.call-update
  312.4 0.0 all-reduce.2.cloned.1.call-start
  312.4 0.1 copy.21
  312.6 4.5 multiply_convert_fusion
  317.1 0.0 all-reduce.2.cloned.1.call-update
  317.1 0.0 reduce-scatter.8.cloned.1.call-start
  317.2 15.2 %fusion = f32[256,2048]{1,0:T(8,128)S(1)} fusion(bf16[2048,7392]{0,1:T(8,128)(2,1)} %param.11, bf16[256,14912]{1,0:T(8,128)(2,1)} %all-gather.4.cloned.1.call-done), kind=kOutput, calls=%fused_computation.4 | convolution fusion | flops 7751073792 | bytes 36175872 | tf_op jit(solution)/shard_map/dot_general | solution.py:18
  332.3 16.1 %fusion.4 = f32[256,2048]{1,0:T(8,128)} fusion(f32[256,2048]{1,0:T(8,128)S(1)} %fusion, bf16[2048,7392]{0,1:T(8,128)(2,1)} %param.10, bf16[256,14912]{1,0:T(8,128)(2,1)} %all-gather.4.cloned.1.call-done), kind=kOutput, calls=%fused_computation.8 | convolution fusion | flops 7751598080 | bytes 38273024 | tf_op jit(solution)/shard_map/dot_general | solution.py:18
  348.4 0.0 reduce-scatter.8.cloned.1.call-update
  348.4 0.0 reduce-scatter.12.cloned.1.call-done
  348.4 0.8 copy.25
  349.3 31.5 %all-gather.6.cloned.1.call-done = bf16[16384,64]{0,1:T(8,128)(2,1)} async-done(((bf16[2048,64]{0,1:T(8,128)(2,1)}), bf16[16384,64]{0,1:T(8,128)(2,1)}) %all-gather.6.cloned.1.call-update) | async-done | bytes 2097168 | tf_op jit(solution)/shard_map/all_gather | solution.py:11
  380.8 2.8 copy.27
  383.6 1.6 bitcast_reduce_fusion
  385.1 0.8 convert_element_type.66
  386.0 104.2 %all-reduce.2.cloned.1.call-done = bf16[16,64,2048]{2,1,0:T(8,128)(2,1)} async-done(((bf16[16,64,2048]{2,1,0:T(8,128)(2,1)}), bf16[16,64,2048]{2,1,0:T(8,128)(2,1)}) %all-reduce.2.cloned.1.call-update) | async-done | bytes 4194320 | tf_op jit(solution)/shard_map/psum | solution.py:109
  490.1 6.7 %convert_element_type.70 = f32[16,64,2048]{2,1,0:T(8,128)} convert(bf16[16,64,2048]{2,1,0:T(8,128)(2,1)} %all-reduce.2.cloned.1.call-done) | non-fusion elementwise | flops 2097152 | bytes 12582912 | tf_op jit(solution)/shard_map/convert_element_type | solution.py:112
  496.8 39.2 %reduce-scatter.8.cloned.1.call-done = f32[64,2048]{1,0:T(8,128)} async-done(((f32[256,2048]{1,0:T(8,128)}), f32[64,2048]{1,0:T(8,128)}) %reduce-scatter.8.cloned.1.call-update) | async-done | bytes 524304 | tf_op jit(solution)/shard_map/reduce_scatter | solution.py:95
  535.9 2.0 fusion.7
  (2 shorter events, 0.0 us)
Async XLA Ops:
  7.2 1.2 copy-start
  7.2 240.0 %reduce-scatter.10.cloned.1.call-start = ((), (), s32[]{:S(2)}) async-start(), calls=%async_computation.7 | async-start | bytes 28672000 | tf_op jit(solution)/shard_map/reduce_scatter | solution.py:43
  24.1 15.9 %copy-start.2 = (bf16[16,64,2048]{2,1,0:T(8,128)(2,1)S(1)}, bf16[16,64,2048]{2,1,0:T(8,128)(2,1)}, u32[]{:S(2)}) copy-start(bf16[16,64,2048]{2,1,0:T(8,128)(2,1)} %param.14) | copy-start | bytes 12582916
  24.1 15.9 %copy-start.3 = (bf16[256,2048]{1,0:T(8,128)(2,1)S(1)}, bf16[256,2048]{1,0:T(8,128)(2,1)}, u32[]{:S(2)}) copy-start(bf16[256,2048]{1,0:T(8,128)(2,1)} %param.9) | copy-start | bytes 3145732
  41.3 15.8 %copy-start.1 = (bf16[2048,64]{0,1:T(8,128)(2,1)S(1)}, bf16[2048,64]{0,1:T(8,128)(2,1)}, u32[]{:S(2)}) copy-start(bf16[2048,64]{0,1:T(8,128)(2,1)} %param.13) | copy-start | bytes 786436
  82.1 226.5 %all-gather.4.cloned.1.call-start = ((), (), s32[]{:S(2)}) async-start(), calls=%async_computation.3 | async-start | bytes 9584640 | tf_op jit(solution)/shard_map/all_gather | solution.py:84
  254.3 94.2 %reduce-scatter.12.cloned.1.call-start = ((), (), s32[]{:S(2)}) async-start(), calls=%async_computation.8 | async-start | bytes 163840
  310.4 70.3 %all-gather.6.cloned.1.call-start = ((), (), s32[]{:S(2)}) async-start(), calls=%async_computation.6 | async-start | bytes 2359296 | tf_op jit(solution)/shard_map/all_gather | solution.py:11
  312.4 177.7 %all-reduce.2.cloned.1.call-start = ((), (), s32[]{:S(2)}) async-start(), calls=%async_computation.5 | async-start | bytes 8388608 | tf_op jit(solution)/shard_map/psum | solution.py:109
  317.1 218.8 %reduce-scatter.8.cloned.1.call-start = ((), (), s32[]{:S(2)}) async-start(), calls=%async_computation.4 | async-start | bytes 2621440 | tf_op jit(solution)/shard_map/reduce_scatter | solution.py:95
Sparse Core Ops, SparseCore 0:
  82.2 164.9 reduce-scatter.9
  254.4 54.1 all-gather.3
  311.4 19.4 reduce-scatter.11
  333.5 47.2 all-gather.5
  383.6 106.4 all-reduce.1
  492.3 43.6 reduce-scatter.7
